TPU v7x, 32 devices: a whole 2x2x4 slice. The times are simulated.
32 devices in a mesh: seq: 16 (over z, x, core), head: 2 (over y).
Axes of the slice: x: 2, y: 2, z: 4, core: 2. Of those that a mesh axis runs over, the one named last changes fastest.
Arguments:
- queries: bfloat16 [8192, 3072], P(('seq', 'head'))
- keys: bfloat16 [8192, 3072], P(('seq', 'head'))
- values: bfloat16 [8192, 3072], P(('seq', 'head')), may hold values from -6 to 6
- kv_blocks: int32 [64, 64], replicated, may hold values from 0 to 63, as said below
- block_counts: int32 [64, 16], replicated, may hold values from 0 to 4, as said below
Outputs:
- attended: bfloat16 [8192, 3072], P(('seq', 'head'))
Inputs may be any that keep to these rules, and one draw needn't show every extreme that they name: `kv_blocks`: slot f * 4 + j names a key block of frame f, as a global block index f * 4 + local; the valid slots of one query block and frame name distinct blocks; slots at or beyond block_counts carry a block of the same frame and no meaning. With e the distance between frame f and the frame of query block b: block_counts[b, f] is 4 where e is 0, at most 2 where e is 1, at most 1 where e is 2, 3 or a power of two, and 0 otherwise; each of these largest values is taken by the first query block of every frame.
All inputs are finite; a program needn't handle non-finite values.
Results may differ from a plain program's by a relative error of at most 0.02.
Values may be sent and summed in bfloat16 or wider, within the bound.
A program may use at most 128 MiB of HBM per device.

v0:
```python
import jax
import jax.numpy as jnp
from jax import lax
from jax.sharding import PartitionSpec as P

HD = 128
BLK = 128
SLOTS = 4


NEG_FILL = -1e30


def from_behind(block, axis, distance):
    devices = range(lax.axis_size(axis))
    route = [(i - distance, i) for i in devices if i - distance in devices]
    return lax.ppermute(block, axis, route)


def rotate_time(matrix, frame_ids):
    row_count = matrix.shape[0]
    head_count = matrix.shape[1] // HD
    per_head = matrix.reshape(row_count, head_count, HD)
    pair_index = jnp.arange(8, dtype=jnp.float32)
    frequency = 256.0 ** (-pair_index / 8.0)
    angles = frame_ids.astype(jnp.float32)[:, None] * frequency[None, :]
    cosine = jnp.cos(angles)[:, None, :]
    sine_part = jnp.sin(angles)[:, None, :]
    pair_view = per_head[:, :, :16].reshape(row_count, head_count, 8, 2)
    even_part = pair_view[..., 0]
    odd_part = pair_view[..., 1]
    turned = jnp.stack(
        [even_part * cosine - odd_part * sine_part, even_part * sine_part + odd_part * cosine],
        axis=-1,
    )
    joined = jnp.concatenate(
        [turned.reshape(row_count, head_count, 16), per_head[:, :, 16:]], axis=2
    )
    return joined.reshape(row_count, head_count * HD)


def signed_distances(frame_count):
    base = [1, 2, 3]
    power = 4
    while power < frame_count:
        base.append(power)
        power = power * 2
    result = [0]
    for step in base:
        result.append(step)
        result.append(-step)
    return result


def slot_cap(distance):
    if distance == 0:
        return SLOTS
    if abs(distance) == 1:
        return 2
    return 1


def block_table(kv_blocks, block_counts, query_frame, key_frame, cap, frame_blocks, frame_count):
    valid = (
        (query_frame >= 0)
        & (query_frame < frame_count)
        & (key_frame >= 0)
        & (key_frame < frame_count)
    )
    query_clip = jnp.clip(query_frame, 0, frame_count - 1)
    key_clip = jnp.clip(key_frame, 0, frame_count - 1)
    row_start = query_clip * frame_blocks
    block_ids = (
        lax.dynamic_slice(kv_blocks, (row_start, key_clip * SLOTS), (frame_blocks, cap))
        - key_clip * frame_blocks
    )
    counts = lax.dynamic_slice(block_counts, (row_start, key_clip), (frame_blocks, 1))[:, 0]
    return (block_ids, jnp.where(valid, counts, 0), valid)


def frame_partial(query_group, key_blocks, value_blocks, block_ids, valid_counts, cap):
    picked_keys = key_blocks[block_ids]
    picked_values = value_blocks[block_ids]
    scores = jnp.einsum(
        "bqhd,bskhd->bhqsk", query_group, picked_keys, preferred_element_type=jnp.float32
    ) * HD ** (-0.5)
    usable = (jnp.arange(cap, dtype=jnp.int32)[None, :] < valid_counts[:, None])[
        :, None, None, :, None
    ]
    masked = jnp.where(usable, scores, NEG_FILL)
    part_max = jnp.max(masked, axis=(3, 4))
    probs = jnp.where(usable, jnp.exp(masked - part_max[..., None, None]), 0.0)
    part_sum = jnp.sum(probs, axis=(3, 4))
    part_num = jnp.einsum(
        "bhqsk,bskhd->bqhd",
        probs.astype(jnp.bfloat16),
        picked_values,
        preferred_element_type=jnp.float32,
    )
    return (part_num.astype(jnp.bfloat16), part_max, part_sum)


def guarded_partial(query_group, key_blocks, value_blocks, block_ids, valid_counts, cap):
    return frame_partial(query_group, key_blocks, value_blocks, block_ids, valid_counts, cap)


def merge_state(state, part):
    run_max, run_sum, run_num = state
    part_num, part_max, part_sum = part
    new_max = jnp.maximum(run_max, part_max)
    old_scale = jnp.exp(run_max - new_max)
    new_scale = jnp.exp(part_max - new_max)
    run_sum = old_scale * run_sum + new_scale * part_sum
    run_num = (
        run_num * jnp.transpose(old_scale, (0, 2, 1))[..., None]
        + part_num.astype(jnp.float32) * jnp.transpose(new_scale, (0, 2, 1))[..., None]
    )
    return (new_max, run_sum, run_num)


def local(queries, keys, values, kv_blocks, block_counts):
    seq_index = lax.axis_index("seq")
    frame_count = lax.axis_size("seq")
    query_slab = lax.all_to_all(queries, "head", split_axis=1, concat_axis=0, tiled=True)
    key_slab, value_slab = (
        lax.all_to_all(keys, "head", split_axis=1, concat_axis=0, tiled=True),
        lax.all_to_all(values, "head", split_axis=1, concat_axis=0, tiled=True),
    )
    frame_tokens = key_slab.shape[0]
    row_width = key_slab.shape[1]
    head_count = row_width // HD
    frame_blocks = frame_tokens // BLK
    frame_ids = jnp.zeros((frame_tokens,), jnp.int32) + seq_index
    query_turned = rotate_time(query_slab.astype(jnp.float32), frame_ids).astype(jnp.bfloat16)
    key_turned = rotate_time(key_slab.astype(jnp.float32), frame_ids).astype(jnp.bfloat16)
    query_group = query_turned.reshape(frame_blocks, BLK, head_count, HD)
    key_blocks = key_turned.reshape(frame_blocks, BLK, head_count, HD)
    value_blocks = value_slab.reshape(frame_blocks, BLK, head_count, HD)
    stat_shape = (frame_blocks, head_count, BLK)
    state = (
        jnp.full(stat_shape, NEG_FILL, jnp.float32),
        jnp.zeros(stat_shape, jnp.float32),
        jnp.zeros((frame_blocks, BLK, head_count, HD), jnp.float32),
    )
    for distance in signed_distances(frame_count):
        cap = slot_cap(distance)
        if distance == 0:
            block_ids, counts, valid = block_table(
                kv_blocks, block_counts, seq_index, seq_index, cap, frame_blocks, frame_count
            )
            part = frame_partial(query_group, key_blocks, value_blocks, block_ids, counts, cap)
        else:
            far_keys, far_values = from_behind((key_blocks, value_blocks), "seq", distance)
            block_ids, counts, valid = block_table(
                kv_blocks,
                block_counts,
                seq_index,
                seq_index - distance,
                cap,
                frame_blocks,
                frame_count,
            )
            part = guarded_partial(query_group, far_keys, far_values, block_ids, counts, cap)
        state = merge_state(state, part)
    denominator = jnp.transpose(state[1], (0, 2, 1))[..., None]
    attended = (state[2] / denominator).reshape(frame_tokens, row_width).astype(jnp.bfloat16)
    return lax.all_to_all(attended, "head", split_axis=0, concat_axis=1, tiled=True)


def solution(mesh):
    in_specs = (
        P(("seq", "head"), None),
        P(("seq", "head"), None),
        P(("seq", "head"), None),
        P(),
        P(),
    )
    out_specs = P(("seq", "head"), None)
    return jax.shard_map(local, mesh=mesh, in_specs=in_specs, out_specs=out_specs, check_vma=False)
```

profile of v0, /device:TPU:24, one launch (start us, length us, event | category | flops | bytes accessed | tf_op | source)
XLA Modules:
  0.0 654.1 jit_solution(9133775101212698396)
XLA Ops:
  9.5 16.3 %all-to-all-done.1 = bf16[256,2,1536]{0,2,1:T(8,128)(2,1)S(1)} async-done(((bf16[256,2,1536]{0,2,1:T(8,128)(2,1)}), bf16[256,2,1536]{0,2,1:T(8,128)(2,1)S(1)}, u32[]{:S(2)}, u32[]{:S(2)}) %all-to-all-start.1) | async-done | bytes 1572896 | tf_op jit(solution)/shard_map/all_to_all | solution.py:126
  35.6 12.6 %all-to-all-done.2 = bf16[256,2,1536]{0,2,1:T(8,128)(2,1)S(1)} async-done(((bf16[256,2,1536]{0,2,1:T(8,128)(2,1)}), bf16[256,2,1536]{0,2,1:T(8,128)(2,1)S(1)}, u32[]{:S(2)}, u32[]{:S(2)}) %all-to-all-start.2) | async-done | bytes 1572896 | tf_op jit(solution)/shard_map/all_to_all | solution.py:127
  54.6 10.7 %copy.203 = bf16[2,256,1536]{1,0,2:T(2,128)(2,1)} copy(bf16[2,256,1536]{1,2,0:T(8,128)(2,1)S(1)} %bitcast.448) | data formatting | bytes 3145728 | tf_op jit(solution)/shard_map/all_to_all | solution.py:127
  65.3 5.2 reshape.374
  81.4 10.7 %copy.195 = bf16[2,256,1536]{1,0,2:T(2,128)(2,1)} copy(bf16[2,256,1536]{1,2,0:T(8,128)(2,1)S(1)} %bitcast.447) | data formatting | bytes 3145728 | tf_op jit(solution)/shard_map/convert_element_type | solution.py:135
  127.8 5.2 collective-permute-start.10
  141.8 5.5 gather_fusion
  159.3 5.6 fusion
  164.9 7.5 %collective-permute-start.7 = (bf16[4,128,12,128]{3,1,2,0:T(8,128)(2,1)S(1)}, bf16[4,128,12,128]{3,1,2,0:T(8,128)(2,1)}, u32[]{:S(2)}, u32[]{:S(2)}) collective-permute-start(bf16[4,128,12,128]{3,1,2,0:T(8,128)(2,1)S(1)} %copy.204), channel_id=1, source_target_pairs={{4,0},{6,2},{8,4},{10,6},{12,8},{14,10},{16,12},{18,14},{20,16},{2... | collective-permute-start | bytes 4718600 | tf_op jit(solution)/shard_map/ppermute | solution.py:17
  174.3 8.9 %collective-permute-start.6 = (bf16[4,128,12,128]{3,1,2,0:T(8,128)(2,1)}, bf16[4,128,12,128]{3,1,2,0:T(8,128)(2,1)}, u32[]{:S(2)}, u32[]{:S(2)}) collective-permute-start(bf16[4,128,12,128]{3,1,2,0:T(8,128)(2,1)} %pad_maximum_fusion.1), channel_id=1, source_target_pairs={{4,0},{6,2},{8,4},{10,6},{12,8},{14,10},{16,12},{18,14},{20,16},{2... | collective-permute-start | bytes 4718600 | tf_op jit(solution)/shard_map/ppermute | solution.py:17
  185.8 11.9 %bitcast_convert_fusion.2 = bf16[4,12,128,128]{3,2,1,0:T(8,128)(2,1)} fusion(f32[4,12,128,512]{2,3,1,0} %get-tuple-element.88, f32[4,12,128]{2,1,0:T(8,128)S(1)} %get-tuple-element.87, pred[4,4]{1,0:T(4,128)(4,1)S(1)} %copy-done.73, bf16[4,4,128,12,128]{4,2,3,1,0:T(8,128)(2,1)} %bitcast.446), kind=kOutput, calls=%fused_computation.84 | convolution fusion | flops 821821440 | bytes 20471824 | tf_op jit(solution)/shard_map/bhqsk,bskhd->bqhd/dot_general | solution.py:94
  199.3 6.6 %fusion.1 = f32[4,12,128]{2,1,0:T(8,128)S(1)} fusion(f32[4,12,128,512]{2,3,1,0} %get-tuple-element.88, f32[4,12,128]{2,1,0:T(8,128)S(1)} %get-tuple-element.87, pred[4,4]{1,0:T(4,128)(4,1)S(1)} %copy-done.73), kind=kLoop, calls=%fused_computation.25 | loop fusion | flops 15722496 | bytes 12632080 | tf_op jit(solution)/shard_map/reduce_sum | solution.py:93
  226.5 60.4 %collective-permute-done.7 = bf16[4,128,12,128]{3,1,2,0:T(8,128)(2,1)} collective-permute-done((bf16[4,128,12,128]{3,1,2,0:T(8,128)(2,1)S(1)}, bf16[4,128,12,128]{3,1,2,0:T(8,128)(2,1)}, u32[]{:S(2)}, u32[]{:S(2)}) %collective-permute-start.7) | collective-permute-done | bytes 1572896 | tf_op jit(solution)/shard_map/ppermute | solution.py:17
  286.9 9.1 %collective-permute-start.19 = (bf16[4,128,12,128]{3,1,2,0:T(8,128)(2,1)S(1)}, bf16[4,128,12,128]{3,1,2,0:T(8,128)(2,1)}, u32[]{:S(2)}, u32[]{:S(2)}) collective-permute-start(bf16[4,128,12,128]{3,1,2,0:T(8,128)(2,1)S(1)} %copy.204), channel_id=1, source_target_pairs={{16,0},{18,2},{20,4},{22,6},{24,8},{26,10},{28,12},{30,14},{17,1},... | collective-permute-start | bytes 4718600 | tf_op jit(solution)/shard_map/ppermute | solution.py:17
  299.4 21.2 %collective-permute-done.6 = bf16[4,128,12,128]{3,1,2,0:T(8,128)(2,1)} collective-permute-done((bf16[4,128,12,128]{3,1,2,0:T(8,128)(2,1)}, bf16[4,128,12,128]{3,1,2,0:T(8,128)(2,1)}, u32[]{:S(2)}, u32[]{:S(2)}) %collective-permute-start.6) | collective-permute-done | bytes 1572896 | tf_op jit(solution)/shard_map/ppermute | solution.py:17
  320.6 7.5 %collective-permute-start.15 = (bf16[4,128,12,128]{3,1,2,0:T(8,128)(2,1)S(1)}, bf16[4,128,12,128]{3,1,2,0:T(8,128)(2,1)}, u32[]{:S(2)}, u32[]{:S(2)}) collective-permute-start(bf16[4,128,12,128]{3,1,2,0:T(8,128)(2,1)S(1)} %copy.204), channel_id=1, source_target_pairs={{8,0},{10,2},{12,4},{14,6},{16,8},{18,10},{20,12},{22,14},{24,16},... | collective-permute-start | bytes 4718600 | tf_op jit(solution)/shard_map/ppermute | solution.py:17
  374.5 52.8 %collective-permute-done.14 = bf16[4,128,12,128]{3,1,2,0:T(8,128)(2,1)} collective-permute-done((bf16[4,128,12,128]{3,1,2,0:T(8,128)(2,1)}, bf16[4,128,12,128]{3,1,2,0:T(8,128)(2,1)}, u32[]{:S(2)}, u32[]{:S(2)}) %collective-permute-start.14) | collective-permute-done | bytes 1572896 | tf_op jit(solution)/shard_map/ppermute | solution.py:17
  454.6 54.1 %collective-permute-done = bf16[4,128,12,128]{3,1,2,0:T(8,128)(2,1)} collective-permute-done((bf16[4,128,12,128]{3,1,2,0:T(8,128)(2,1)}, bf16[4,128,12,128]{3,1,2,0:T(8,128)(2,1)}, u32[]{:S(2)}, u32[]{:S(2)}) %collective-permute-start) | collective-permute-done | bytes 1572896 | tf_op jit(solution)/shard_map/ppermute | solution.py:17
  508.8 8.9 %collective-permute-start.3 = (bf16[4,128,12,128]{3,1,2,0:T(8,128)(2,1)S(1)}, bf16[4,128,12,128]{3,1,2,0:T(8,128)(2,1)}, u32[]{:S(2)}, u32[]{:S(2)}) collective-permute-start(bf16[4,128,12,128]{3,1,2,0:T(8,128)(2,1)S(1)} %copy.204), channel_id=1, source_target_pairs={{2,0},{4,2},{6,4},{8,6},{10,8},{12,10},{14,12},{16,14},{18,16},{20... | collective-permute-start | bytes 4718600 | tf_op jit(solution)/shard_map/ppermute | solution.py:17
  536.9 5.2 fusion.13
  559.8 22.2 %collective-permute-done.17 = bf16[4,128,12,128]{3,1,2,0:T(8,128)(2,1)} collective-permute-done((bf16[4,128,12,128]{3,1,2,0:T(8,128)(2,1)S(1)}, bf16[4,128,12,128]{3,1,2,0:T(8,128)(2,1)}, u32[]{:S(2)}, u32[]{:S(2)}) %collective-permute-start.17) | collective-permute-done | bytes 1572896 | tf_op jit(solution)/shard_map/ppermute | solution.py:17
  603.9 7.2 %bitcast_convert_fusion.1 = bf16[4,12,128,128]{3,2,1,0:T(8,128)(2,1)} fusion(f32[4,12,128,256]{2,3,1,0} %get-tuple-element.86, f32[4,12,128]{2,1,0:T(8,128)S(1)} %get-tuple-element.85, pred[4,2]{1,0:T(4,128)(4,1)S(1)} %copy-done.54, bf16[4,2,128,12,128]{4,2,3,1,0:T(8,128)(2,1)} %bitcast.453), kind=kOutput, calls=%fused_computation.79 | convolution fusion | flops 411303936 | bytes 11034632 | tf_op jit(solution)/shard_map/bhqsk,bskhd->bqhd/dot_general | solution.py:94
  618.1 9.8 %fusion.23 = bf16[4,128,12,128]{1,3,2,0:T(8,128)(2,1)S(1)} fusion(bf16[4,12,128,128]{3,2,1,0:T(8,128)(2,1)} %convolution_convert_fusion.1, bf16[4,12,128,128]{3,2,1,0:T(8,128)(2,1)} %convolution_convert_fusion.2, bf16[4,12,128,128]{3,2,1,0:T(8,128)(2,1)} %convolution_convert_fusion.3, bf16[4,12,128,128]{3,2,1,0:T(8,128)(2,1)} %convolution_convert_fusion.4, ...), kind=kOutput, calls=%fused_computation.49 | convolution fusion | flops 241434624 | bytes 22609924 | tf_op jit(solution)/shard_map/bhqsk,bskhd->bqhd/dot_general | solution.py:94
  630.4 21.5 %all_to_all.58 = bf16[2,256,1536]{1,2,0:T(8,128)(2,1)S(1)} all-to-all(bf16[2,256,1536]{1,2,0:T(8,128)(2,1)S(1)} %copy.248), channel_id=1, replica_groups=mesh['seq'=16,'head'=2] {'head'}, dimensions={0} | all-to-all | bytes 3145728 | tf_op jit(solution)/shard_map/all_to_all | solution.py:167
  (308 shorter events, 265.8 us)
Async XLA Ops:
  2.7 23.2 %all-to-all-start.1 = ((bf16[256,2,1536]{0,2,1:T(8,128)(2,1)}), bf16[256,2,1536]{0,2,1:T(8,128)(2,1)S(1)}, u32[]{:S(2)}, u32[]{:S(2)}) async-start(bf16[256,2,1536]{0,2,1:T(8,128)(2,1)} %bitcast.3), calls=%async_computation.1 | async-start | bytes 3145728 | tf_op jit(solution)/shard_map/all_to_all | solution.py:126
  25.9 22.3 %all-to-all-start.2 = ((bf16[256,2,1536]{0,2,1:T(8,128)(2,1)}), bf16[256,2,1536]{0,2,1:T(8,128)(2,1)S(1)}, u32[]{:S(2)}, u32[]{:S(2)}) async-start(bf16[256,2,1536]{0,2,1:T(8,128)(2,1)} %bitcast.449), calls=%async_computation.2 | async-start | bytes 3145728 | tf_op jit(solution)/shard_map/all_to_all | solution.py:127
  48.1 48.0 %all-to-all-start = ((bf16[256,2,1536]{0,2,1:T(8,128)(2,1)}), bf16[256,2,1536]{0,2,1:T(8,128)(2,1)}, u32[]{:S(2)}, u32[]{:S(2)}) async-start(bf16[256,2,1536]{0,2,1:T(8,128)(2,1)} %bitcast.450), calls=%async_computation | async-start | bytes 3145728 | tf_op jit(solution)/shard_map/all_to_all | solution.py:124
  73.2 62.4 %collective-permute-start.13 = (bf16[4,128,12,128]{3,1,2,0:T(8,128)(2,1)S(1)}, bf16[4,128,12,128]{3,1,2,0:T(8,128)(2,1)}, u32[]{:S(2)}, u32[]{:S(2)}) collective-permute-start(bf16[4,128,12,128]{3,1,2,0:T(8,128)(2,1)S(1)} %copy.204), channel_id=1, source_target_pairs={{0,8},{2,10},{4,12},{6,14},{8,16},{10,18},{12,20},{14,22},{16,24},... | collective-permute-start | bytes 4718600 | tf_op jit(solution)/shard_map/ppermute | solution.py:17
  74.5 90.4 %collective-permute-start.11 = (bf16[4,128,12,128]{3,1,2,0:T(8,128)(2,1)S(1)}, bf16[4,128,12,128]{3,1,2,0:T(8,128)(2,1)}, u32[]{:S(2)}, u32[]{:S(2)}) collective-permute-start(bf16[4,128,12,128]{3,1,2,0:T(8,128)(2,1)S(1)} %copy.204), channel_id=1, source_target_pairs={{6,0},{8,2},{10,4},{12,6},{14,8},{16,10},{18,12},{20,14},{22,16},{... | collective-permute-start | bytes 4718600 | tf_op jit(solution)/shard_map/ppermute | solution.py:17
  76.5 95.9 %collective-permute-start.9 = (bf16[4,128,12,128]{3,1,2,0:T(8,128)(2,1)S(1)}, bf16[4,128,12,128]{3,1,2,0:T(8,128)(2,1)}, u32[]{:S(2)}, u32[]{:S(2)}) collective-permute-start(bf16[4,128,12,128]{3,1,2,0:T(8,128)(2,1)S(1)} %copy.204), channel_id=1, source_target_pairs={{0,6},{2,8},{4,10},{6,12},{8,14},{10,16},{12,18},{14,20},{16,22},{... | collective-permute-start | bytes 4718600 | tf_op jit(solution)/shard_map/ppermute | solution.py:17
  126.5 47.8 %collective-permute-start.12 = (bf16[4,128,12,128]{3,1,2,0:T(8,128)(2,1)}, bf16[4,128,12,128]{3,1,2,0:T(8,128)(2,1)}, u32[]{:S(2)}, u32[]{:S(2)}) collective-permute-start(bf16[4,128,12,128]{3,1,2,0:T(8,128)(2,1)} %pad_maximum_fusion.1), channel_id=1, source_target_pairs={{0,8},{2,10},{4,12},{6,14},{8,16},{10,18},{12,20},{14,22},{16,24},... | collective-permute-start | bytes 4718600 | tf_op jit(solution)/shard_map/ppermute | solution.py:17
  127.8 55.5 %collective-permute-start.10 = (bf16[4,128,12,128]{3,1,2,0:T(8,128)(2,1)}, bf16[4,128,12,128]{3,1,2,0:T(8,128)(2,1)}, u32[]{:S(2)}, u32[]{:S(2)}) collective-permute-start(bf16[4,128,12,128]{3,1,2,0:T(8,128)(2,1)} %pad_maximum_fusion.1), channel_id=1, source_target_pairs={{6,0},{8,2},{10,4},{12,6},{14,8},{16,10},{18,12},{20,14},{22,16},{... | collective-permute-start | bytes 4718600 | tf_op jit(solution)/shard_map/ppermute | solution.py:17
  135.6 62.0 %collective-permute-start.8 = (bf16[4,128,12,128]{3,1,2,0:T(8,128)(2,1)}, bf16[4,128,12,128]{3,1,2,0:T(8,128)(2,1)}, u32[]{:S(2)}, u32[]{:S(2)}) collective-permute-start(bf16[4,128,12,128]{3,1,2,0:T(8,128)(2,1)} %pad_maximum_fusion.1), channel_id=1, source_target_pairs={{0,6},{2,8},{4,10},{6,12},{8,14},{10,16},{12,18},{14,20},{16,22},{... | collective-permute-start | bytes 4718600 | tf_op jit(solution)/shard_map/ppermute | solution.py:17
  164.9 122.0 %collective-permute-start.7 = (bf16[4,128,12,128]{3,1,2,0:T(8,128)(2,1)S(1)}, bf16[4,128,12,128]{3,1,2,0:T(8,128)(2,1)}, u32[]{:S(2)}, u32[]{:S(2)}) collective-permute-start(bf16[4,128,12,128]{3,1,2,0:T(8,128)(2,1)S(1)} %copy.204), channel_id=1, source_target_pairs={{4,0},{6,2},{8,4},{10,6},{12,8},{14,10},{16,12},{18,14},{20,16},{2... | collective-permute-start | bytes 4718600 | tf_op jit(solution)/shard_map/ppermute | solution.py:17
  172.4 159.2 %collective-permute-start.5 = (bf16[4,128,12,128]{3,1,2,0:T(8,128)(2,1)S(1)}, bf16[4,128,12,128]{3,1,2,0:T(8,128)(2,1)}, u32[]{:S(2)}, u32[]{:S(2)}) collective-permute-start(bf16[4,128,12,128]{3,1,2,0:T(8,128)(2,1)S(1)} %copy.204), channel_id=1, source_target_pairs={{0,4},{2,6},{4,8},{6,10},{8,12},{10,14},{12,16},{14,18},{16,20},{1... | collective-permute-start | bytes 4718600 | tf_op jit(solution)/shard_map/ppermute | solution.py:17
  174.3 146.3 %collective-permute-start.6 = (bf16[4,128,12,128]{3,1,2,0:T(8,128)(2,1)}, bf16[4,128,12,128]{3,1,2,0:T(8,128)(2,1)}, u32[]{:S(2)}, u32[]{:S(2)}) collective-permute-start(bf16[4,128,12,128]{3,1,2,0:T(8,128)(2,1)} %pad_maximum_fusion.1), channel_id=1, source_target_pairs={{4,0},{6,2},{8,4},{10,6},{12,8},{14,10},{16,12},{18,14},{20,16},{2... | collective-permute-start | bytes 4718600 | tf_op jit(solution)/shard_map/ppermute | solution.py:17
  183.3 154.2 %collective-permute-start.4 = (bf16[4,128,12,128]{3,1,2,0:T(8,128)(2,1)}, bf16[4,128,12,128]{3,1,2,0:T(8,128)(2,1)}, u32[]{:S(2)}, u32[]{:S(2)}) collective-permute-start(bf16[4,128,12,128]{3,1,2,0:T(8,128)(2,1)} %pad_maximum_fusion.1), channel_id=1, source_target_pairs={{0,4},{2,6},{4,8},{6,10},{8,12},{10,14},{12,16},{14,18},{16,20},{1... | collective-permute-start | bytes 4718600 | tf_op jit(solution)/shard_map/ppermute | solution.py:17
  197.6 159.0 %collective-permute-start.16 = (bf16[4,128,12,128]{3,1,2,0:T(8,128)(2,1)}, bf16[4,128,12,128]{3,1,2,0:T(8,128)(2,1)}, u32[]{:S(2)}, u32[]{:S(2)}) collective-permute-start(bf16[4,128,12,128]{3,1,2,0:T(8,128)(2,1)} %pad_maximum_fusion.1), channel_id=1, source_target_pairs={{0,16},{2,18},{4,20},{6,22},{8,24},{10,26},{12,28},{14,30},{1,17},... | collective-permute-start | bytes 4718600 | tf_op jit(solution)/shard_map/ppermute | solution.py:17
  286.9 327.6 %collective-permute-start.19 = (bf16[4,128,12,128]{3,1,2,0:T(8,128)(2,1)S(1)}, bf16[4,128,12,128]{3,1,2,0:T(8,128)(2,1)}, u32[]{:S(2)}, u32[]{:S(2)}) collective-permute-start(bf16[4,128,12,128]{3,1,2,0:T(8,128)(2,1)S(1)} %copy.204), channel_id=1, source_target_pairs={{16,0},{18,2},{20,4},{22,6},{24,8},{26,10},{28,12},{30,14},{17,1},... | collective-permute-start | bytes 4718600 | tf_op jit(solution)/shard_map/ppermute | solution.py:17
  320.6 226.9 %collective-permute-start.15 = (bf16[4,128,12,128]{3,1,2,0:T(8,128)(2,1)S(1)}, bf16[4,128,12,128]{3,1,2,0:T(8,128)(2,1)}, u32[]{:S(2)}, u32[]{:S(2)}) collective-permute-start(bf16[4,128,12,128]{3,1,2,0:T(8,128)(2,1)S(1)} %copy.204), channel_id=1, source_target_pairs={{8,0},{10,2},{12,4},{14,6},{16,8},{18,10},{20,12},{22,14},{24,16},... | collective-permute-start | bytes 4718600 | tf_op jit(solution)/shard_map/ppermute | solution.py:17
  331.6 199.9 %collective-permute-start.18 = (bf16[4,128,12,128]{3,1,2,0:T(8,128)(2,1)}, bf16[4,128,12,128]{3,1,2,0:T(8,128)(2,1)}, u32[]{:S(2)}, u32[]{:S(2)}) collective-permute-start(bf16[4,128,12,128]{3,1,2,0:T(8,128)(2,1)} %pad_maximum_fusion.1), channel_id=1, source_target_pairs={{16,0},{18,2},{20,4},{22,6},{24,8},{26,10},{28,12},{30,14},{17,1},... | collective-permute-start | bytes 4718600 | tf_op jit(solution)/shard_map/ppermute | solution.py:17
  337.4 89.8 %collective-permute-start.14 = (bf16[4,128,12,128]{3,1,2,0:T(8,128)(2,1)}, bf16[4,128,12,128]{3,1,2,0:T(8,128)(2,1)}, u32[]{:S(2)}, u32[]{:S(2)}) collective-permute-start(bf16[4,128,12,128]{3,1,2,0:T(8,128)(2,1)} %pad_maximum_fusion.1), channel_id=1, source_target_pairs={{8,0},{10,2},{12,4},{14,6},{16,8},{18,10},{20,12},{22,14},{24,16},... | collective-permute-start | bytes 4718600 | tf_op jit(solution)/shard_map/ppermute | solution.py:17
  356.6 88.7 %collective-permute-start.2 = (bf16[4,128,12,128]{3,1,2,0:T(8,128)(2,1)}, bf16[4,128,12,128]{3,1,2,0:T(8,128)(2,1)}, u32[]{:S(2)}, u32[]{:S(2)}) collective-permute-start(bf16[4,128,12,128]{3,1,2,0:T(8,128)(2,1)} %pad_maximum_fusion.1), channel_id=1, source_target_pairs={{2,0},{4,2},{6,4},{8,6},{10,8},{12,10},{14,12},{16,14},{18,16},{20... | collective-permute-start | bytes 4718600 | tf_op jit(solution)/shard_map/ppermute | solution.py:17
  374.5 58.4 %copy-start.60 = (pred[4]{0:T(512)(128)(4,1)S(1)}, pred[4]{0:T(512)(128)(4,1)}, u32[]{:S(2)}) copy-start(pred[4]{0:T(512)(128)(4,1)} %get-tuple-element.57) | copy-start | bytes 16
  427.3 81.5 %collective-permute-start = (bf16[4,128,12,128]{3,1,2,0:T(8,128)(2,1)}, bf16[4,128,12,128]{3,1,2,0:T(8,128)(2,1)}, u32[]{:S(2)}, u32[]{:S(2)}) collective-permute-start(bf16[4,128,12,128]{3,1,2,0:T(8,128)(2,1)} %pad_maximum_fusion.1), channel_id=1, source_target_pairs={{0,2},{2,4},{4,6},{6,8},{8,10},{10,12},{12,14},{14,16},{16,18},{18... | collective-permute-start | bytes 4718600 | tf_op jit(solution)/shard_map/ppermute | solution.py:17
  445.3 136.7 %collective-permute-start.17 = (bf16[4,128,12,128]{3,1,2,0:T(8,128)(2,1)S(1)}, bf16[4,128,12,128]{3,1,2,0:T(8,128)(2,1)}, u32[]{:S(2)}, u32[]{:S(2)}) collective-permute-start(bf16[4,128,12,128]{3,1,2,0:T(8,128)(2,1)S(1)} %copy.204), channel_id=1, source_target_pairs={{0,16},{2,18},{4,20},{6,22},{8,24},{10,26},{12,28},{14,30},{1,17},... | collective-permute-start | bytes 4718600 | tf_op jit(solution)/shard_map/ppermute | solution.py:17
  508.8 87.0 %collective-permute-start.3 = (bf16[4,128,12,128]{3,1,2,0:T(8,128)(2,1)S(1)}, bf16[4,128,12,128]{3,1,2,0:T(8,128)(2,1)}, u32[]{:S(2)}, u32[]{:S(2)}) collective-permute-start(bf16[4,128,12,128]{3,1,2,0:T(8,128)(2,1)S(1)} %copy.204), channel_id=1, source_target_pairs={{2,0},{4,2},{6,4},{8,6},{10,8},{12,10},{14,12},{16,14},{18,16},{20... | collective-permute-start | bytes 4718600 | tf_op jit(solution)/shard_map/ppermute | solution.py:17
  531.5 68.3 %collective-permute-start.1 = (bf16[4,128,12,128]{3,1,2,0:T(8,128)(2,1)S(1)}, bf16[4,128,12,128]{3,1,2,0:T(8,128)(2,1)}, u32[]{:S(2)}, u32[]{:S(2)}) collective-permute-start(bf16[4,128,12,128]{3,1,2,0:T(8,128)(2,1)S(1)} %copy.204), channel_id=1, source_target_pairs={{0,2},{2,4},{4,6},{6,8},{8,10},{10,12},{12,14},{14,16},{16,18},{18... | collective-permute-start | bytes 4718600 | tf_op jit(solution)/shard_map/ppermute | solution.py:17
  (76 other events, 357.8 us)
where the time goes:
time: 662 us; the launch traced here: 654 us
  waiting for transfers between devices  240 us (36%)
  local copies, waits for them, and re-layouts  169 us (26%)
  matrix products  92.9 us (14%)
  starting transfers between devices  89.1 us (13%)
  other arithmetic  40.5 us (6%)
  blocking collectives  21.5 us (3%)
    ppermute x20, waiting for transfers between devices, from_behind(): return lax.ppermute(block, axis, route)  211 us
    ppermute x20, starting transfers between devices, from_behind(): return lax.ppermute(block, axis, route)  77.1 us
    dot_general x11, matrix products, frame_partial(): jnp.einsum('bhqsk,bskhd->bqhd', probs.astype(jnp.bfloat16), picked_values...  52 us
    gather x14, local copies, waits for them, and re-layouts, frame_partial(): picked_keys = key_blocks[block_ids]  51.4 us
    gather x11, local copies, waits for them, and re-layouts, frame_partial(): picked_values = value_blocks[block_ids]  37.4 us
    dot_general x8, matrix products, frame_partial(): jnp.einsum('bqhd,bskhd->bhqsk', query_group, picked_keys, preferred_eleme...  27.8 us
    reduce_sum x7, other arithmetic, frame_partial(): part_sum = jnp.sum(probs, axis=(3, 4))  23.8 us
    all_to_all x1, blocking collectives, local(): lax.all_to_all(attended, 'head', split_axis=0, concat_axis=1, tiled=True)  21.5 us
  transfers between devices with their start and end apart: 23, of which 7 were waited for; matrix products, arithmetic and copies ran while one was open for 43% of the time, Pallas kernels for 0%

commit v1 on v0

v1 whole, which is shorter than its diff:
```python
import functools
import math

import jax
import jax.numpy as jnp
import numpy as np
from jax import lax
from jax.experimental import pallas as pl
from jax.experimental.pallas import tpu as pltpu
from jax.sharding import PartitionSpec as P

HD = 128
BLK = 128
SLOTS = 4
MESH = pl.DeviceIdType.MESH
EXP2_SCALE = HD ** (-0.5) * math.log2(math.e)


def distances(frames):
    result = [1, 2, 3]
    power = 4
    while power < frames:
        result.append(power)
        power = power * 2
    return result


def turn_table(frames):
    lane = np.arange(HD)
    frequency = (256.0 ** (-(lane // 2) / 8.0)).astype(np.float32)
    angle = np.arange(frames, dtype=np.float32)[:, None] * frequency[None, :]
    cosine = np.cos(angle.astype(np.float64))
    sine = np.sin(angle.astype(np.float64))
    turned = lane < 16
    even = lane % 2 == 0
    table = np.zeros((frames, 8, HD), np.float32)
    table[:, 0] = np.where(turned, cosine, 1.0)
    table[:, 1] = np.where(turned & even, -sine, 0.0)
    table[:, 2] = np.where(turned & ~even, sine, 0.0)
    return table


def chunk_count(heads):
    for count in (4, 3, 2):
        if heads % count == 0:
            return count
    return 1


def kernel(plan, kv_ref, count_ref, turn_ref, q_ref, k_ref, v_hbm, out_hbm, *scratch):
    frames, groups, rows, heads, chunks, offsets = plan
    width = heads // chunks * HD
    group_width = heads * HD
    chunk_heads = heads // chunks
    tokens = rows * groups
    frame_blocks = tokens // BLK
    n_off = len(offsets)
    scratch = list(scratch)

    def take(n):
        head, scratch[:] = scratch[:n], scratch[n:]
        return head

    kv = {0: take(chunks)}
    for o in offsets:
        kv[o] = take(chunks)
    q_all = take(chunks)
    att = take(chunks)
    stage_k, stage_q, scores = take(3)
    in_send, in_recv, local_sem, seq_send, seq_recv, out_send, out_recv, out_local = take(8)
    where_of = {o: i for i, o in enumerate(offsets)}

    frame = lax.axis_index("seq")
    me = lax.axis_index("head")
    core = frame % 2
    parity = (frame // 2) % 2
    sibling = frame + 1 - 2 * core
    partner = frame + 2 - 4 * parity
    my_rows = pl.ds(pl.multiple_of(me * rows, rows), rows)
    whole_blocks = rows % BLK == 0

    def rows_of(buffer, which, group):
        if whole_blocks:
            return buffer.at[which, pl.ds(group * (rows // BLK), rows // BLK)]
        first = group * rows
        return buffer.at[which, first // BLK, pl.ds(pl.multiple_of(first % BLK, rows), rows), :]

    def has(o):
        return frame + o < frames if o > 0 else frame + o >= 0

    steps = [4]
    while steps[-1] * 4 < frames:
        steps.append(steps[-1] * 2)

    barrier = pltpu.get_barrier_semaphore()

    def greet(seq, head):
        pl.semaphore_signal(barrier, inc=1, device_id=(seq, head), device_id_type=MESH)

    greet(sibling, me)
    greet(partner, me)
    expected = 2 + groups - 1
    for s in steps:
        for o in (-s, s):
            @pl.when(has(o))
            def _(o=o):
                greet(frame + o, me)

            expected = expected + jnp.where(has(o), 1, 0)
    for r in range(1, groups):
        greet(frame, (me + r) % groups)
    pl.semaphore_wait(barrier, expected)

    def turn(src, dst, column, blocked):
        table = turn_ref[frame]
        cosine, up, down = table[0:1, :], table[1:2, :], table[2:3, :]
        piece = min(rows, 32)

        @pl.loop(0, rows // piece)
        def _(i):
            at = pl.ds(pl.multiple_of(i * piece, piece), piece)
            for h in range(chunk_heads):
                col = pl.ds(pl.multiple_of(column + h * HD, HD), HD)
                x = src[at, col].astype(jnp.float32)
                y = x * cosine + pltpu.roll(x, HD - 1, 1) * up + pltpu.roll(x, 1, 1) * down
                y = y.astype(jnp.bfloat16)
                lanes = slice(h * HD, (h + 1) * HD)
                if blocked and whole_blocks:
                    inner = pl.ds(pl.multiple_of(i * piece % BLK, piece), piece)
                    dst[i * piece // BLK, inner, lanes] = y
                else:
                    dst[at, lanes] = y

    def column_of(group, c):
        return pl.multiple_of(group * group_width + c * width, HD)

    def value_columns(group, c):
        col = pl.ds(column_of(group, c), width)
        return v_hbm.at[:, :, col] if whole_blocks else v_hbm.at[:, col]

    def in_copy(c, r, what):
        target = (me + r) % groups
        if what == 0:
            src = stage_k.at[r - 1, c]
        elif what == 1:
            src = value_columns(target, c)
        else:
            src = stage_q.at[r - 1, c]
        dst = q_all[c].at[my_rows, :] if what == 2 else rows_of(kv[0][c], what, me)
        return pltpu.make_async_remote_copy(
            src_ref=src, dst_ref=dst, send_sem=in_send.at[c, r - 1, what],
            recv_sem=in_recv.at[c, r - 1, what], device_id=(frame, target), device_id_type=MESH)

    def in_wait(c, r, what):
        source = (me + groups - r) % groups
        at = pl.ds(pl.multiple_of(source * rows, rows), rows)
        dst = q_all[c].at[at, :] if what == 2 else rows_of(kv[0][c], what, source)
        pltpu.make_async_remote_copy(
            src_ref=dst, dst_ref=dst, send_sem=in_send.at[c, r - 1, what],
            recv_sem=in_recv.at[c, r - 1, what], device_id=(frame, source),
            device_id_type=MESH).wait_recv()

    def local_value(c):
        return pltpu.make_async_copy(
            value_columns(me, c), rows_of(kv[0][c], 1, me), local_sem.at[c])

    def enter(c):
        for r in range(1, groups):
            turn(k_ref, stage_k.at[r - 1, c], column_of((me + r) % groups, c), True)
            in_copy(c, r, 0).start()
            in_copy(c, r, 1).start()
        local_value(c).start()
        turn(k_ref, rows_of(kv[0][c], 0, me), column_of(me, c), True)

    def enter_queries(c):
        for r in range(1, groups):
            turn(q_ref, stage_q.at[r - 1, c], column_of((me + r) % groups, c), False)
            in_copy(c, r, 2).start()
        turn(q_ref, q_all[c].at[my_rows, :], column_of(me, c), False)

    def copy_of(c, slot, held, there, target):
        return pltpu.make_async_remote_copy(
            src_ref=kv[held][c], dst_ref=kv[there][c], send_sem=seq_send.at[c, slot],
            recv_sem=seq_recv.at[c, where_of[there]], device_id=(target, me), device_id_type=MESH)

    def wait_for(c, o, condition):
        @pl.when(condition)
        def _():
            copy_of(c, 0, o, o, sibling).wait_recv()

    even_core, odd_core = core == 0, core == 1
    low, high = parity == 0, parity == 1
    always = frame >= 0
    own_routes = [
        (has(4), 0, -4, frame + 4),
        (has(-4), 0, 4, frame - 4),
        (low, 0, -2, partner),
        (high, 0, 2, partner),
        (even_core, 0, -1, sibling),
        (odd_core, 0, 1, sibling),
    ]
    after_four = [
        (low & has(4), 4, 2, partner),
        (high & has(-4), -4, -2, partner),
        (even_core & has(4), 4, 3, sibling),
        (odd_core & has(-4), -4, -3, sibling),
    ]
    if 8 < frames:
        after_four = [
            (has(-4) & has(4), -4, -8, frame + 4),
            (has(-4) & has(4), 4, 8, frame - 4),
        ] + after_four
    after_two = [
        (low & even_core, 2, 1, sibling),
        (low & odd_core, 2, 3, sibling),
        (high & even_core, -2, -3, sibling),
        (high & odd_core, -2, -1, sibling),
    ]
    after_far_two = [
        (low & even_core & has(-2), -2, -3, sibling),
        (low & odd_core & has(-2), -2, -1, sibling),
        (high & even_core & has(2), 2, 1, sibling),
        (high & odd_core & has(2), 2, 3, sibling),
    ]
    after_power = []
    power = 8
    while power * 2 < frames:
        after_power.append((power, [
            (has(-power) & has(power), -power, -2 * power, frame + power),
            (has(-power) & has(power), power, 2 * power, frame - power),
        ]))
        power = power * 2
    routes = own_routes + after_four + after_two + after_far_two
    for _, extra in after_power:
        routes = routes + extra
    slot_of = {id(route): i for i, route in enumerate(routes)}

    def send(c, some):
        for route in some:
            condition, held, there, target = route

            @pl.when(condition)
            def _(route=route, held=held, there=there, target=target):
                copy_of(c, slot_of[id(route)], held, there, target).start()

    def send_own(c):
        for r in range(1, groups):
            in_wait(c, r, 0)
            in_wait(c, r, 1)
        local_value(c).wait()
        send(c, own_routes)

    def forward(c):
        wait_for(c, -4, has(-4))
        wait_for(c, 4, has(4))
        send(c, after_four)
        wait_for(c, 2, low)
        wait_for(c, -2, high)
        send(c, after_two)

    def forward_far(c):
        wait_for(c, -2, low & has(-2))
        wait_for(c, 2, high & has(2))
        send(c, after_far_two)
        for power, some in after_power:
            wait_for(c, -power, has(-power))
            wait_for(c, power, has(power))
            send(c, some)

    waited = [-4, 4, -2, 2]
    for power, _ in after_power:
        waited += [-power, power]

    slots = []
    for o in offsets:
        slots += [(o, j) for j in range(2 if abs(o) == 1 else 1)]
    pairs = [slots[i:i + 2] for i in range(0, len(slots), 2)]
    own_pairs = tokens // (2 * BLK)

    def attend(c):
        for o in offsets:
            if o not in waited:
                wait_for(c, o, has(o))
        for r in range(1, groups):
            in_wait(c, r, 2)

        @pl.loop(0, frame_blocks)
        def _(b):
            at = pl.ds(pl.multiple_of(b * BLK, BLK), BLK)
            table_row = frame * frame_blocks + b
            start = {}
            bound = {}
            for o, j in slots:
                there = jnp.clip(frame + o, 0, frames - 1)
                block = kv_ref[table_row, there * SLOTS + j] - there * frame_blocks
                block = jnp.clip(block, 0, frame_blocks - 1)
                start[o, j] = block
                usable = jnp.where(has(o), count_ref[table_row, there], 0) > j
                bound[o, j] = jnp.where(usable, jnp.float32(jnp.inf), jnp.float32(-jnp.inf))
            for h in range(chunk_heads):
                col = slice(h * HD, (h + 1) * HD)
                query = q_all[c][at, col]

                def side(pair, which):
                    return jnp.concatenate(
                        [kv[o][c][which, start[o, j], :, col] for o, j in pair], axis=0)

                def own_side(i, which):
                    return kv[0][c][which, 2 * i:2 * i + 2, :, col].reshape(2 * BLK, HD)

                top = None
                for i in range(own_pairs + len(pairs)):
                    if i < own_pairs:
                        key = own_side(i, 0)
                    else:
                        key = side(pairs[i - own_pairs], 0)
                    s = lax.dot_general(query, key, (((1,), (1,)), ((), ())),
                                        preferred_element_type=jnp.float32)
                    left, right = s[:, :BLK], s[:, BLK:]
                    if i >= own_pairs:
                        one, two = pairs[i - own_pairs]
                        left = jnp.minimum(left, bound[one])
                        right = jnp.minimum(right, bound[two])
                    scores[h, i, :, :BLK] = left
                    scores[h, i, :, BLK:] = right
                    both = jnp.maximum(left, right)
                    top = both if top is None else jnp.maximum(top, both)
                top = jnp.max(top, axis=1, keepdims=True)
                total = None
                out = None
                for i in range(own_pairs + len(pairs)):
                    p = jnp.exp2((scores[h, i] - top) * EXP2_SCALE)
                    part = p[:, :BLK] + p[:, BLK:]
                    total = part if total is None else total + part
                    if i < own_pairs:
                        value = own_side(i, 1)
                    else:
                        value = side(pairs[i - own_pairs], 1)
                    term = jnp.dot(p.astype(jnp.bfloat16), value, preferred_element_type=jnp.float32)
                    out = term if out is None else out + term
                total = jnp.sum(total, axis=1, keepdims=True)
                att[c][at, col] = (out / total).astype(jnp.bfloat16)

    def out_copy(c, r):
        target = (me + r) % groups
        at = pl.ds(pl.multiple_of(target * rows, rows), rows)
        return pltpu.make_async_remote_copy(
            src_ref=att[c].at[at, :], dst_ref=out_hbm.at[:, pl.ds(column_of(me, c), width)],
            send_sem=out_send.at[c, r - 1], recv_sem=out_recv.at[c, r - 1],
            device_id=(frame, target), device_id_type=MESH)

    def out_wait(c, r):
        source = (me + groups - r) % groups
        at = out_hbm.at[:, pl.ds(column_of(source, c), width)]
        pltpu.make_async_remote_copy(
            src_ref=at, dst_ref=at, send_sem=out_send.at[c, r - 1],
            recv_sem=out_recv.at[c, r - 1], device_id=(frame, source),
            device_id_type=MESH).wait_recv()

    def local_out(c):
        return pltpu.make_async_copy(
            att[c].at[my_rows, :], out_hbm.at[:, pl.ds(column_of(me, c), width)], out_local.at[c])

    def leave(c):
        for r in range(1, groups):
            out_copy(c, r).start()
        local_out(c).start()

    enter(0)
    for c in range(chunks):
        if c + 1 < chunks:
            enter(c + 1)
        send_own(c)
    for c in range(chunks):
        enter_queries(c)
    for o in offsets:
        @pl.when(jnp.logical_not(has(o)))
        def _(o=o):
            @pl.loop(0, frame_blocks)
            def _(i):
                for c in range(chunks):
                    for which in range(2):
                        kv[o][c][which, i] = jnp.zeros((BLK, width), jnp.bfloat16)

    forward(0)
    for c in range(chunks):
        if c + 1 < chunks:
            forward(c + 1)
        forward_far(c)
        attend(c)
        leave(c)

    for c in range(chunks):
        for r in range(1, groups):
            for what in range(3):
                in_copy(c, r, what).wait_send()
            out_copy(c, r).wait_send()
            out_wait(c, r)
        local_out(c).wait()
        for route in routes:
            condition, held, there, target = route

            @pl.when(condition)
            def _(route=route, held=held, there=there, target=target):
                copy_of(c, slot_of[id(route)], held, there, target).wait_send()


def local(queries, keys, values, kv_blocks, block_counts):
    frames = lax.axis_size("seq")
    groups = lax.axis_size("head")
    rows, model = queries.shape
    heads = model // HD // groups
    chunks = chunk_count(heads)
    width = heads // chunks * HD
    tokens = rows * groups
    offsets = [o for d in distances(frames) for o in (-d, d)]
    n_slots = len(offsets) + 2
    n_pairs = tokens // (2 * BLK) + n_slots // 2
    plan = (frames, groups, rows, heads, chunks, tuple(offsets))
    n_routes = 18 + 2 * len(offsets)
    lead = (rows // BLK, BLK) if rows % BLK == 0 else (rows,)
    chunk = pltpu.VMEM((2, tokens // BLK, BLK, width), jnp.bfloat16)
    flat = pltpu.VMEM((tokens, width), jnp.bfloat16)
    stage = pltpu.VMEM((max(groups - 1, 1), chunks, rows, width), jnp.bfloat16)
    stage_k = pltpu.VMEM((max(groups - 1, 1), chunks) + lead + (width,), jnp.bfloat16)
    sem = pltpu.SemaphoreType.DMA
    others = max(groups - 1, 1)
    return pl.pallas_call(
        functools.partial(kernel, plan),
        out_shape=jax.ShapeDtypeStruct((rows, model), jnp.bfloat16),
        in_specs=[
            pl.BlockSpec(memory_space=pltpu.SMEM),
            pl.BlockSpec(memory_space=pltpu.SMEM),
            pl.BlockSpec(memory_space=pltpu.VMEM),
            pl.BlockSpec(memory_space=pltpu.VMEM),
            pl.BlockSpec(memory_space=pltpu.VMEM),
            pl.BlockSpec(memory_space=pl.ANY),
        ],
        out_specs=pl.BlockSpec(memory_space=pl.ANY),
        scratch_shapes=[chunk] * (chunks * (1 + len(offsets))) + [flat] * (2 * chunks) + [
            stage_k,
            stage,
            pltpu.VMEM((heads // chunks, n_pairs, BLK, 2 * BLK), jnp.float32),
            sem((chunks, others, 3)),
            sem((chunks, others, 3)),
            sem((chunks,)),
            sem((chunks, n_routes)),
            sem((chunks, len(offsets))),
            sem((chunks, others)),
            sem((chunks, others)),
            sem((chunks,)),
        ],
        compiler_params=pltpu.CompilerParams(
            collective_id=0, has_side_effects=True, vmem_limit_bytes=60 * 1024 * 1024
        ),
    )(kv_blocks, block_counts, jnp.asarray(turn_table(frames)), queries, keys,
      values.reshape(lead + (model,)))


def solution(mesh):
    in_specs = (
        P(("seq", "head"), None),
        P(("seq", "head"), None),
        P(("seq", "head"), None),
        P(),
        P(),
    )
    out_specs = P(("seq", "head"), None)
    return jax.shard_map(local, mesh=mesh, in_specs=in_specs, out_specs=out_specs, check_vma=False)
```

time: 662 us -> 170 us (0.26)
  waiting for transfers between devices: 240 us -> 0 us
  local copies, waits for them, and re-layouts: 169 us -> 4.05 us
  Pallas kernels: 0 us -> 164 us
  matrix products: 92.9 us -> 0 us
  starting transfers between devices: 89.1 us -> 0 us
  other arithmetic: 40.5 us -> 0 us
  blocking collectives: 21.5 us -> 0 us
    ppermute x20 -> x0, waiting for transfers between devices: 211 us -> none  [from_behind(): return lax.ppermute(block, axis, route)]
    pallas_call x0 -> x1, Pallas kernels: none -> 164 us  [local(): pl.pallas_call(functools.partial(kernel, plan), out_shape=jax.ShapeDtypeS...]
    gather x25 -> x0, local copies, waits for them, and re-layouts: 88.8 us -> none  [the longest x14 51.4 us: frame_partial(): picked_keys = key_blocks[block_ids]]
    dot_general x19 -> x0, matrix products: 79.8 us -> none  [the longest x11 52 us: frame_partial(): jnp.einsum('bhqsk,bskhd->bqhd', probs.astype(jnp.bfloat16), picked_values...]
    ppermute x20 -> x0, starting transfers between devices: 77.1 us -> none  [from_behind(): return lax.ppermute(block, axis, route)]
    all_to_all x3 -> x0, waiting for transfers between devices: 28.9 us -> none  [the longest x1 16.3 us: local(): lax.all_to_all(keys, 'head', split_axis=1, concat_axis=0, tiled=True)]
    reduce_sum x7 -> x0, other arithmetic: 23.8 us -> none  [frame_partial(): part_sum = jnp.sum(probs, axis=(3, 4))]
    convert_element_type x7 -> x0, local copies, waits for them, and re-layouts: 23.6 us -> none  [the longest x2 13.5 us: local(): key_slab.astype(jnp.float32)]
  transfers between devices with their start and end apart: 23 -> 0, of which waited for: 7 -> 0; matrix products, arithmetic and copies ran while one was open for 43% -> 0% of each run, Pallas kernels for 0% -> 0%
where the time goes in v1:
time: 170 us; the launch traced here: 168 us
  Pallas kernels  164 us (96%)
  local copies, waits for them, and re-layouts  4.05 us (2%)
    pallas_call x1, Pallas kernels, local(): pl.pallas_call(functools.partial(kernel, plan), out_shape=jax.ShapeDtypeS...  164 us
    unnamed x2, local copies, waits for them, and re-layouts  4.05 us

profile of v1, /device:TPU:24, one launch (start us, length us, event | category | flops | bytes accessed | tf_op | source)
XLA Modules:
  0.0 168.3 jit_solution(2635976051819572027)
XLA Ops:
  0.0 1.4 copy.7.count_ref
  1.4 164.3 %shard_map.64 = bf16[256,3072]{1,0:T(8,128)(2,1)} custom-call(s32[64,64]{1,0:T(8,128)} %kv_ref.1, s32[64,16]{1,0:T(8,128)} %copy.7.count_ref, f32[16,8,128]{2,1,0:T(8,128)} %constant.2.clone.turn_ref, bf16[256,3072]{1,0:T(8,128)(2,1)} %q_ref.1, bf16[256,3072]{1,0:T(8,128)(2,1)} %k_ref.1, bf16[2,128,3072]{2,1,0:T(8,128)(2,1)} %bitcast.1), custom_call_target="tpu_custom_call" | custom-call | tf_op jit(solution)/shard_map/pallas_call | solution.py:428
  165.7 2.7 %copy.9 = bf16[256,3072]{1,0:T(8,128)(2,1)} copy(bf16[256,3072]{1,0:T(8,128)(2,1)} %shard_map.64) | data formatting | bytes 3145728

commit v2 on v1

--- a/solution.py
+++ b/solution.py
@@ -40,18 +40,20 @@
     return table
 
 
-def chunk_count(heads):
-    for count in (4, 3, 2):
-        if heads % count == 0:
-            return count
-    return 1
-
-
-def kernel(plan, kv_ref, count_ref, turn_ref, q_ref, k_ref, v_hbm, out_hbm, *scratch):
-    frames, groups, rows, heads, chunks, offsets = plan
-    width = heads // chunks * HD
+def chunk_sizes(heads):
+    if heads < 6:
+        return (1,) * heads
+    middle = heads - 6
+    rest = (middle % 3,) if middle % 3 else ()
+    return (1, 2) + (3,) * (middle // 3) + rest + (2, 1)
+
+
+def kernel(plan, kv_ref, count_ref, turn_ref, q_hbm, k_hbm, v_hbm, out_hbm, *scratch):
+    frames, groups, rows, heads, sizes, offsets = plan
+    chunks = len(sizes)
     group_width = heads * HD
-    chunk_heads = heads // chunks
+    widths = [size * HD for size in sizes]
+    begins = [sum(widths[:c]) for c in range(chunks)]
     tokens = rows * groups
     frame_blocks = tokens // BLK
     n_off = len(offsets)
@@ -66,8 +68,8 @@
         kv[o] = take(chunks)
     q_all = take(chunks)
     att = take(chunks)
-    stage_k, stage_q, scores = take(3)
-    in_send, in_recv, local_sem, seq_send, seq_recv, out_send, out_recv, out_local = take(8)
+    q_ref, k_ref, stage_k, stage_q, scores = take(5)
+    in_send, in_recv, local_sem, seq_send, seq_recv, out_send, out_recv, out_local, load_sem = take(9)
     where_of = {o: i for i, o in enumerate(offsets)}
 
     frame = lax.axis_index("seq")
@@ -92,6 +94,11 @@
     while steps[-1] * 4 < frames:
         steps.append(steps[-1] * 2)
 
+    load_k = pltpu.make_async_copy(k_hbm, k_ref, load_sem.at[0])
+    load_q = pltpu.make_async_copy(q_hbm, q_ref, load_sem.at[1])
+    load_k.start()
+    load_q.start()
+
     barrier = pltpu.get_barrier_semaphore()
 
     def greet(seq, head):
@@ -111,7 +118,7 @@
         greet(frame, (me + r) % groups)
     pl.semaphore_wait(barrier, expected)
 
-    def turn(src, dst, column, blocked):
+    def turn(src, dst, column, c, blocked):
         table = turn_ref[frame]
         cosine, up, down = table[0:1, :], table[1:2, :], table[2:3, :]
         piece = min(rows, 32)
@@ -119,7 +126,7 @@
         @pl.loop(0, rows // piece)
         def _(i):
             at = pl.ds(pl.multiple_of(i * piece, piece), piece)
-            for h in range(chunk_heads):
+            for h in range(sizes[c]):
                 col = pl.ds(pl.multiple_of(column + h * HD, HD), HD)
                 x = src[at, col].astype(jnp.float32)
                 y = x * cosine + pltpu.roll(x, HD - 1, 1) * up + pltpu.roll(x, 1, 1) * down
@@ -132,20 +139,24 @@
                     dst[at, lanes] = y
 
     def column_of(group, c):
-        return pl.multiple_of(group * group_width + c * width, HD)
+        return pl.multiple_of(group * group_width + begins[c], HD)
+
+    def staged(buffer, r, c, blocked):
+        col = pl.ds(begins[c], widths[c])
+        return buffer.at[r - 1, :, :, col] if blocked and whole_blocks else buffer.at[r - 1, :, col]
 
     def value_columns(group, c):
-        col = pl.ds(column_of(group, c), width)
+        col = pl.ds(column_of(group, c), widths[c])
         return v_hbm.at[:, :, col] if whole_blocks else v_hbm.at[:, col]
 
     def in_copy(c, r, what):
         target = (me + r) % groups
         if what == 0:
-            src = stage_k.at[r - 1, c]
+            src = staged(stage_k, r, c, True)
         elif what == 1:
             src = value_columns(target, c)
         else:
-            src = stage_q.at[r - 1, c]
+            src = staged(stage_q, r, c, False)
         dst = q_all[c].at[my_rows, :] if what == 2 else rows_of(kv[0][c], what, me)
         return pltpu.make_async_remote_copy(
             src_ref=src, dst_ref=dst, send_sem=in_send.at[c, r - 1, what],
@@ -166,17 +177,17 @@
 
     def enter(c):
         for r in range(1, groups):
-            turn(k_ref, stage_k.at[r - 1, c], column_of((me + r) % groups, c), True)
+            turn(k_ref, staged(stage_k, r, c, True), column_of((me + r) % groups, c), c, True)
             in_copy(c, r, 0).start()
             in_copy(c, r, 1).start()
         local_value(c).start()
-        turn(k_ref, rows_of(kv[0][c], 0, me), column_of(me, c), True)
+        turn(k_ref, rows_of(kv[0][c], 0, me), column_of(me, c), c, True)
 
     def enter_queries(c):
         for r in range(1, groups):
-            turn(q_ref, stage_q.at[r - 1, c], column_of((me + r) % groups, c), False)
+            turn(q_ref, staged(stage_q, r, c, False), column_of((me + r) % groups, c), c, False)
             in_copy(c, r, 2).start()
-        turn(q_ref, q_all[c].at[my_rows, :], column_of(me, c), False)
+        turn(q_ref, q_all[c].at[my_rows, :], column_of(me, c), c, False)
 
     def copy_of(c, slot, held, there, target):
         return pltpu.make_async_remote_copy(
@@ -295,9 +306,9 @@
                 block = kv_ref[table_row, there * SLOTS + j] - there * frame_blocks
                 block = jnp.clip(block, 0, frame_blocks - 1)
                 start[o, j] = block
-                usable = jnp.where(has(o), count_ref[table_row, there], 0) > j
+                usable = jnp.where(has(o), count_ref[there, table_row], 0) > j
                 bound[o, j] = jnp.where(usable, jnp.float32(jnp.inf), jnp.float32(-jnp.inf))
-            for h in range(chunk_heads):
+            for h in range(sizes[c]):
                 col = slice(h * HD, (h + 1) * HD)
                 query = q_all[c][at, col]
 
@@ -345,13 +356,13 @@
         target = (me + r) % groups
         at = pl.ds(pl.multiple_of(target * rows, rows), rows)
         return pltpu.make_async_remote_copy(
-            src_ref=att[c].at[at, :], dst_ref=out_hbm.at[:, pl.ds(column_of(me, c), width)],
+            src_ref=att[c].at[at, :], dst_ref=out_hbm.at[:, pl.ds(column_of(me, c), widths[c])],
             send_sem=out_send.at[c, r - 1], recv_sem=out_recv.at[c, r - 1],
             device_id=(frame, target), device_id_type=MESH)
 
     def out_wait(c, r):
         source = (me + groups - r) % groups
-        at = out_hbm.at[:, pl.ds(column_of(source, c), width)]
+        at = out_hbm.at[:, pl.ds(column_of(source, c), widths[c])]
         pltpu.make_async_remote_copy(
             src_ref=at, dst_ref=at, send_sem=out_send.at[c, r - 1],
             recv_sem=out_recv.at[c, r - 1], device_id=(frame, source),
@@ -359,18 +370,20 @@
 
     def local_out(c):
         return pltpu.make_async_copy(
-            att[c].at[my_rows, :], out_hbm.at[:, pl.ds(column_of(me, c), width)], out_local.at[c])
+            att[c].at[my_rows, :], out_hbm.at[:, pl.ds(column_of(me, c), widths[c])], out_local.at[c])
 
     def leave(c):
         for r in range(1, groups):
             out_copy(c, r).start()
         local_out(c).start()
 
+    load_k.wait()
     enter(0)
     for c in range(chunks):
         if c + 1 < chunks:
             enter(c + 1)
         send_own(c)
+    load_q.wait()
     for c in range(chunks):
         enter_queries(c)
     for o in offsets:
@@ -380,7 +393,7 @@
             def _(i):
                 for c in range(chunks):
                     for which in range(2):
-                        kv[o][c][which, i] = jnp.zeros((BLK, width), jnp.bfloat16)
+                        kv[o][c][which, i] = jnp.zeros((BLK, widths[c]), jnp.bfloat16)
 
     forward(0)
     for c in range(chunks):
@@ -410,19 +423,21 @@
     groups = lax.axis_size("head")
     rows, model = queries.shape
     heads = model // HD // groups
-    chunks = chunk_count(heads)
-    width = heads // chunks * HD
+    sizes = chunk_sizes(heads)
+    chunks = len(sizes)
     tokens = rows * groups
     offsets = [o for d in distances(frames) for o in (-d, d)]
     n_slots = len(offsets) + 2
     n_pairs = tokens // (2 * BLK) + n_slots // 2
-    plan = (frames, groups, rows, heads, chunks, tuple(offsets))
+    plan = (frames, groups, rows, heads, sizes, tuple(offsets))
     n_routes = 18 + 2 * len(offsets)
     lead = (rows // BLK, BLK) if rows % BLK == 0 else (rows,)
-    chunk = pltpu.VMEM((2, tokens // BLK, BLK, width), jnp.bfloat16)
-    flat = pltpu.VMEM((tokens, width), jnp.bfloat16)
-    stage = pltpu.VMEM((max(groups - 1, 1), chunks, rows, width), jnp.bfloat16)
-    stage_k = pltpu.VMEM((max(groups - 1, 1), chunks) + lead + (width,), jnp.bfloat16)
+    blocks = [pltpu.VMEM((2, tokens // BLK, BLK, size * HD), jnp.bfloat16) for size in sizes]
+    flats = [pltpu.VMEM((tokens, size * HD), jnp.bfloat16) for size in sizes]
+    group_width = heads * HD
+    whole = pltpu.VMEM((rows, model), jnp.bfloat16)
+    stage_q = pltpu.VMEM((max(groups - 1, 1), rows, group_width), jnp.bfloat16)
+    stage_k = pltpu.VMEM((max(groups - 1, 1),) + lead + (group_width,), jnp.bfloat16)
     sem = pltpu.SemaphoreType.DMA
     others = max(groups - 1, 1)
     return pl.pallas_call(
@@ -432,15 +447,17 @@
             pl.BlockSpec(memory_space=pltpu.SMEM),
             pl.BlockSpec(memory_space=pltpu.SMEM),
             pl.BlockSpec(memory_space=pltpu.VMEM),
-            pl.BlockSpec(memory_space=pltpu.VMEM),
-            pl.BlockSpec(memory_space=pltpu.VMEM),
+            pl.BlockSpec(memory_space=pl.ANY),
+            pl.BlockSpec(memory_space=pl.ANY),
             pl.BlockSpec(memory_space=pl.ANY),
         ],
         out_specs=pl.BlockSpec(memory_space=pl.ANY),
-        scratch_shapes=[chunk] * (chunks * (1 + len(offsets))) + [flat] * (2 * chunks) + [
+        scratch_shapes=blocks * (1 + len(offsets)) + flats * 2 + [
+            whole,
+            whole,
             stage_k,
-            stage,
-            pltpu.VMEM((heads // chunks, n_pairs, BLK, 2 * BLK), jnp.float32),
+            stage_q,
+            pltpu.VMEM((max(sizes), n_pairs, BLK, 2 * BLK), jnp.float32),
             sem((chunks, others, 3)),
             sem((chunks, others, 3)),
             sem((chunks,)),
@@ -449,11 +466,12 @@
             sem((chunks, others)),
             sem((chunks, others)),
             sem((chunks,)),
+            sem((2,)),
         ],
         compiler_params=pltpu.CompilerParams(
             collective_id=0, has_side_effects=True, vmem_limit_bytes=60 * 1024 * 1024
         ),
-    )(kv_blocks, block_counts, jnp.asarray(turn_table(frames)), queries, keys,
+    )(kv_blocks, block_counts.T, jnp.asarray(turn_table(frames)), queries, keys,
       values.reshape(lead + (model,)))
 
 

time: 170 us -> 161 us (0.947); the launches traced: 168 us -> 161 us
  Pallas kernels: 164 us -> 158 us
    pallas_call x1, Pallas kernels: 164 us -> 158 us  [local(): pl.pallas_call(functools.partial(kernel, plan), out_shape=jax.ShapeDtypeS...]
    unnamed x2 -> x1, local copies, waits for them, and re-layouts: 4.05 us -> 2.65 us
where the time goes in v2:
time: 161 us
  Pallas kernels  158 us (98%)
  local copies, waits for them, and re-layouts  2.65 us (2%)
    pallas_call x1, Pallas kernels, local(): pl.pallas_call(functools.partial(kernel, plan), out_shape=jax.ShapeDtypeS...  158 us

profile of v2, /device:TPU:24, one launch (start us, length us, event | category | flops | bytes accessed | tf_op | source)
XLA Modules:
  0.0 161.1 jit_solution(15604312970248653037)
XLA Ops:
  0.0 158.4 %shard_map.64 = bf16[256,3072]{1,0:T(8,128)(2,1)} custom-call(s32[64,64]{1,0:T(8,128)} %kv_ref.1, s32[16,64]{1,0:T(8,128)} %bitcast.3, f32[16,8,128]{2,1,0:T(8,128)} %constant.2.clone.turn_ref, bf16[256,3072]{1,0:T(8,128)(2,1)} %q_hbm.1, bf16[256,3072]{1,0:T(8,128)(2,1)} %k_hbm.1, bf16[2,128,3072]{2,1,0:T(8,128)(2,1)} %bitcast.2), custom_call_target="tpu_custom_call" | custom-call | tf_op jit(solution)/shard_map/pallas_call | solution.py:443
  158.4 2.7 %copy.8 = bf16[256,3072]{1,0:T(8,128)(2,1)} copy(bf16[256,3072]{1,0:T(8,128)(2,1)} %shard_map.64) | data formatting | bytes 3145728
